TPU v7x, 32 devices: a whole 2x2x4 slice. The times are simulated.
32 devices in a mesh: query: 4 (over y, x), cand: 2 (over core), tensor: 4 (over z).
Axes of the slice: x: 2, y: 2, z: 4, core: 2. Of those that a mesh axis runs over, the one named last changes fastest.
Arguments:
- cand_states: bfloat16 [8192, 2048], P(('query', 'cand'), 'tensor'), parts along dimension 0, may hold values from -6 to 6
- prefix_states: bfloat16 [256, 2048], P(('query', 'cand'), 'tensor'), parts along dimension 0, may hold values from -6 to 6
- norm_gain: float32 [2048], replicated, may hold values from 0.5 to 1.5
- w_query: bfloat16 [2048, 1024], P(None, 'tensor'), may hold values from -1 to 1
- w_key: bfloat16 [2048, 256], P(None, 'tensor'), may hold values from -1 to 1
- w_value: bfloat16 [2048, 256], P(None, 'tensor'), may hold values from -0.125 to 0.125
- w_out: bfloat16 [1024, 2048], P('tensor'), may hold values from -1.5 to 1.5
- cand_lengths: int32 [64], P(('query', 'cand')), parts along dimension 0, may hold values from 32 to 128, as said below
Outputs:
- attn_out: bfloat16 [8192, 2048], P(('query', 'cand', 'tensor')), parts along dimension 0
There are 4 independent parts, one for each index of `query`. A program takes and returns all parts, laid end to end along the dimension named above; an argument that names none is the same for every part. Nothing has to cross between parts.
Inputs may be any that keep to these rules, and one draw needn't show every extreme that they name: `cand_lengths`: some candidate has all 128 slots live.
All inputs are finite; a program needn't handle non-finite values.
Results may differ from a plain program's by a relative error of at most 0.013.
Values may be sent and summed in bfloat16 or wider, within the bound.
No kernel may reach another device: no remote copies, remote signals or barrier semaphores. Data moves between devices by JAX's collectives and lax.ppermute only.
A program may use at most 64 MiB of HBM per device.

v0:
```python
import jax
import jax.numpy as jnp
from jax import lax
from jax.sharding import PartitionSpec as P

epsilon = 1e-06
theta_base = 10000.0


def rotate(values, positions):
    half_size = values.shape[-1] // 2
    frequency = theta_base ** (-jnp.arange(half_size, dtype=jnp.float32) * 2.0 / values.shape[-1])
    angles = positions.astype(jnp.float32)[:, None] * frequency[None, :]
    cosine = jnp.cos(angles)
    sine_part = jnp.sin(angles)
    lower_half = values[:, :half_size]
    upper_half = values[:, half_size:]
    return jnp.concatenate(
        [
            lower_half * cosine - upper_half * sine_part,
            upper_half * cosine + lower_half * sine_part,
        ],
        axis=-1,
    )


def normalize(states, norm_gain):
    values = states.astype(jnp.float32)
    square = jnp.mean(values * values, axis=-1, keepdims=True)
    return (values * lax.rsqrt(square + epsilon) * norm_gain[None, :]).astype(jnp.bfloat16)


def self_scores_of(queries, cand_keys):
    scores = jnp.einsum("cqd,ckd->cqk", queries, cand_keys, preferred_element_type=jnp.float32)
    slots = jnp.arange(scores.shape[1], dtype=jnp.int32)
    causal = slots[:, None] >= slots[None, :]
    return jnp.where(causal[None], scores, -jnp.inf)


def body(cand_states, prefix_states, norm_gain, w_query, w_key, w_value, w_out, cand_lengths):
    cand_full, prefix_full = (
        lax.all_gather(cand_states, "tensor", axis=1, tiled=True),
        lax.all_gather(prefix_states, "tensor", axis=1, tiled=True),
    )
    normed_cand = normalize(cand_full, norm_gain)
    normed_prefix = normalize(prefix_full, norm_gain)
    cand_count = cand_lengths.shape[0]
    cand_len = cand_full.shape[0] // cand_count
    prefix_rows = prefix_full.shape[0]
    cand_groups = lax.axis_size("cand")
    tensor_size = lax.axis_size("tensor")
    prefix_len = prefix_rows * cand_groups
    head_size = w_query.shape[1]
    cand_pos = prefix_len + jnp.tile(jnp.arange(cand_len, dtype=jnp.int32), cand_count)
    cand_key = jnp.dot(normed_cand, w_key, preferred_element_type=jnp.float32).astype(jnp.bfloat16)
    cand_value = jnp.dot(normed_cand, w_value, preferred_element_type=jnp.float32).astype(
        jnp.bfloat16
    )
    prefix_key = jnp.dot(normed_prefix, w_key, preferred_element_type=jnp.float32).astype(
        jnp.bfloat16
    )
    prefix_value = jnp.dot(normed_prefix, w_value, preferred_element_type=jnp.float32).astype(
        jnp.bfloat16
    )
    query_rows = rotate(
        jnp.dot(normed_cand, w_query, preferred_element_type=jnp.float32), cand_pos
    ) * head_size ** (-0.5)
    queries = query_rows.astype(jnp.bfloat16).reshape(cand_count, cand_len, head_size)
    cand_key, cand_value = (
        lax.all_gather(cand_key, "tensor", axis=1, tiled=True),
        lax.all_gather(cand_value, "tensor", axis=1, tiled=True),
    )
    key_pieces, value_pieces = (
        lax.all_gather(prefix_key, ("cand", "tensor"), axis=0, tiled=True),
        lax.all_gather(prefix_value, ("cand", "tensor"), axis=0, tiled=True),
    )

    def arrange(pieces):
        blocks = pieces.reshape(cand_groups, tensor_size, prefix_rows, pieces.shape[1])
        return blocks.transpose(0, 2, 1, 3).reshape(prefix_len, pieces.shape[1] * tensor_size)

    prefix_pos = jnp.arange(prefix_len, dtype=jnp.int32)
    prefix_keys = rotate(arrange(key_pieces).astype(jnp.float32), prefix_pos).astype(jnp.bfloat16)
    prefix_values = arrange(value_pieces)
    cand_keys = (
        rotate(cand_key.astype(jnp.float32), cand_pos)
        .astype(jnp.bfloat16)
        .reshape(cand_count, cand_len, head_size)
    )
    cand_values = cand_value.reshape(cand_count, cand_len, head_size)
    self_scores = self_scores_of(queries, cand_keys)
    prefix_scores = jnp.einsum(
        "cqd,kd->cqk", queries, prefix_keys, preferred_element_type=jnp.float32
    )
    highest = jnp.maximum(self_scores.max(-1), prefix_scores.max(-1))
    self_weights = jnp.exp(self_scores - highest[..., None])
    prefix_weights = jnp.exp(prefix_scores - highest[..., None])
    divisor = self_weights.sum(-1) + prefix_weights.sum(-1)
    summed = jnp.einsum(
        "cqk,ckd->cqd",
        self_weights.astype(jnp.bfloat16),
        cand_values,
        preferred_element_type=jnp.float32,
    )
    summed = summed + jnp.einsum(
        "cqk,kd->cqd",
        prefix_weights.astype(jnp.bfloat16),
        prefix_values,
        preferred_element_type=jnp.float32,
    )
    slots = jnp.arange(cand_len, dtype=jnp.int32)
    live_rows = slots[None, :] < cand_lengths[:, None]
    head_rows = jnp.where(live_rows[..., None], summed / divisor[..., None], 0.0)
    head_rows = head_rows.reshape(cand_count * cand_len, head_size).astype(jnp.bfloat16)
    row_count = head_rows.shape[0] // tensor_size
    all_heads = lax.all_to_all(head_rows, "tensor", split_axis=0, concat_axis=1, tiled=True)
    full_out = lax.all_gather(w_out, "tensor", axis=0, tiled=True)
    summed_out = jnp.zeros((row_count, full_out.shape[1]), jnp.float32)
    for head_index in range(tensor_size):
        head_term = jnp.dot(
            all_heads[:, head_index * head_size : (head_index + 1) * head_size],
            full_out[head_index * head_size : (head_index + 1) * head_size],
            preferred_element_type=jnp.float32,
        )
        summed_out = summed_out + lax.optimization_barrier(head_term.astype(jnp.bfloat16)).astype(
            jnp.float32
        )
    return summed_out.astype(jnp.bfloat16)


def solution(mesh):
    in_specs = (
        P(("query", "cand"), "tensor"),
        P(("query", "cand"), "tensor"),
        P(),
        P(None, "tensor"),
        P(None, "tensor"),
        P(None, "tensor"),
        P("tensor", None),
        P(("query", "cand")),
    )
    out_specs = P(("query", "cand", "tensor"), None)
    return jax.shard_map(body, mesh=mesh, in_specs=in_specs, out_specs=out_specs, check_vma=False)
```

profile of v0, /device:TPU:0, one launch (start us, length us, event | category | flops | bytes accessed | tf_op | source)
XLA Modules:
  0.0 214.7 jit_solution(11699257511544938787)
XLA Ops:
  6.5 0.0 copy-start
  6.5 0.0 copy-start.6
  6.5 0.0 copy-start.7
  6.5 0.0 all-gather.3.cloned.1.call-start
  6.5 0.7 all-gather.3.cloned.1.call-update
  7.3 0.0 all-gather.5.cloned.1.call-start
  7.3 0.7 all-gather.5.cloned.1.call-update
  8.0 15.3 %all_gather.23 = bf16[32,2048]{1,0:T(8,128)(2,1)S(1)} all-gather(bf16[32,512]{1,0:T(8,128)(2,1)} %param.9), channel_id=1, replica_groups=mesh['query'=4,'cand'=2,'tensor'=4] {'tensor'}, dimensions={1}, use_global_device_ids=true | all-gather | bytes 163840 | tf_op jit(solution)/shard_map/all_gather | solution.py:43
  23.3 0.1 fusion.30
  23.5 1.2 convolution_convert_fusion.7
  24.7 26.7 %all_gather.24 = bf16[256,64]{1,0:T(8,128)(2,1)S(1)} all-gather(bf16[32,64]{1,0:T(8,128)(2,1)S(1)} %convolution_convert_fusion.7), channel_id=1, replica_groups=mesh['query'=4,'cand'=2,'tensor'=4] {'cand','tensor'}, dimensions={0}, use_global_device_ids=true | all-gather | bytes 36864 | tf_op jit(solution)/shard_map/all_gather | solution.py:74
  51.4 0.1 copy.21
  51.5 0.1 reshape.111
  51.6 1.2 convolution_convert_fusion.6
  52.8 27.9 %all_gather.26 = bf16[256,64]{1,0:T(8,128)(2,1)S(1)} all-gather(bf16[32,64]{1,0:T(8,128)(2,1)S(1)} %convolution_convert_fusion.6), channel_id=1, replica_groups=mesh['query'=4,'cand'=2,'tensor'=4] {'cand','tensor'}, dimensions={0}, use_global_device_ids=true | all-gather | bytes 36864 | tf_op jit(solution)/shard_map/all_gather | solution.py:75
  80.8 0.1 reshape.114
  81.0 0.0 copy-done.7
  81.0 0.1 iota_compare_fusion.1
  81.1 0.2 fusion.51
  81.3 13.3 %all-gather.3.cloned.1.call-done = bf16[1024,2048]{1,0:T(8,128)(2,1)} async-done(((bf16[1024,512]{1,0:T(8,128)(2,1)}), bf16[1024,2048]{1,0:T(8,128)(2,1)}) %all-gather.3.cloned.1.call-update) | async-done | bytes 4194320 | tf_op jit(solution)/shard_map/all_gather | solution.py:42
  94.6 0.0 copy-start.2
  94.6 3.2 %fusion = f32[1024]{0:T(1024)S(1)} fusion(bf16[1024,2048]{1,0:T(8,128)(2,1)} %all-gather.3.cloned.1.call-done), kind=kLoop, calls=%fused_computation.2 | loop fusion | flops 6290432 | bytes 4198400 | tf_op jit(solution)/shard_map/reduce_sum | solution.py:29
  97.8 0.0 copy-done.6
  97.8 0.2 copy-done.2
  98.0 0.0 copy-start.4
  98.0 1.0 fusion.2
  99.0 0.0 copy-start.1
  99.1 2.0 copy-done.1
  101.0 0.0 copy-done.4
  101.0 0.0 copy-start.5
  101.0 1.4 convolution_convert_fusion.5
  102.4 21.4 %all_gather.22 = bf16[1024,256]{0,1:T(8,128)(2,1)S(1)} all-gather(bf16[1024,64]{0,1:T(8,128)(2,1)S(1)} %convolution_convert_fusion.5), channel_id=1, replica_groups=mesh['query'=4,'cand'=2,'tensor'=4] {'tensor'}, dimensions={1}, use_global_device_ids=true | all-gather | bytes 655360 | tf_op jit(solution)/shard_map/all_gather | solution.py:70
  123.8 0.2 copy.20
  124.0 0.1 convert_element_type.144
  124.1 0.0 copy-done.5
  124.1 3.6 %convolution_convert_fusion.4 = bf16[1024,64]{0,1:T(8,128)(2,1)S(1)} fusion(bf16[1024,2048]{1,0:T(8,128)(2,1)} %copy-done.1, bf16[2048,64]{0,1:T(8,128)(2,1)S(1)} %copy-done.5), kind=kOutput, calls=%fused_computation.15 | convolution fusion | flops 268500992 | bytes 4587520 | tf_op jit(solution)/shard_map/dot_general | solution.py:56
  127.7 21.3 %all_gather.25 = bf16[1024,256]{0,1:T(8,128)(2,1)S(1)} all-gather(bf16[1024,64]{0,1:T(8,128)(2,1)S(1)} %convolution_convert_fusion.4), channel_id=1, replica_groups=mesh['query'=4,'cand'=2,'tensor'=4] {'tensor'}, dimensions={1}, use_global_device_ids=true | all-gather | bytes 655360 | tf_op jit(solution)/shard_map/all_gather | solution.py:71
  149.0 0.2 copy.27
  149.2 0.0 copy-done
  149.2 3.5 %fusion.67 = f32[1024,256]{1,0:T(8,128)S(1)} fusion(bf16[1024,2048]{1,0:T(8,128)(2,1)} %copy-done.1, bf16[2048,256]{1,0:T(8,128)(2,1)S(1)} %copy-done), kind=kOutput, calls=%fused_computation.92 | convolution fusion | flops 1073741824 | bytes 6291456 | tf_op jit(solution)/shard_map/dot_general | solution.py:66
  152.7 2.5 %fusion.19 = (f32[1024,128]{1,0:T(8,128)S(1)}, f32[1024,128]{1,0:T(8,128)S(1)}, bf16[1024,128]{1,0:T(8,128)(2,1)S(1)}, bf16[1024,128]{1,0:T(8,128)(2,1)S(1)}) fusion(f32[1024,256]{1,0:T(8,128)S(1)} %fusion.67, f32[128]{0:T(128)S(1)} %multiply_power_fusion, f32[1024]{0:T(1024)S(1)} %convert_bitcast_fusion.1, f32[1024,256]{1,0:T(8,128)S(1)} %convert_element_type.144), kind=kLoop, calls=%fused_computation.35 | loop fusion | flops 1966080 | bytes 3674624 | tf_op jit(solution)/shard_map/sub | solution.py:20
  155.2 0.3 fusion.66
  155.5 0.3 fusion.65
  155.8 0.1 fusion.36
  155.9 0.1 fusion.28
  156.0 0.3 fusion.33
  156.3 0.4 fusion.5
  156.8 1.0 copy.25
  157.8 5.3 %all-to-all-start = ((bf16[4,256,256]{1,2,0:T(8,128)(2,1)}), bf16[4,256,256]{1,2,0:T(8,128)(2,1)S(1)}, u32[]{:S(2)}, u32[]{:S(2)}) async-start(bf16[4,256,256]{1,2,0:T(8,128)(2,1)} %copy.25), calls=%async_computation | async-start | bytes 1048576 | tf_op jit(solution)/shard_map/all_to_all | solution.py:116
  163.1 38.6 %all-gather.5.cloned.1.call-done = bf16[1024,2048]{1,0:T(8,128)(2,1)} async-done(((bf16[256,2048]{1,0:T(8,128)(2,1)}), bf16[1024,2048]{1,0:T(8,128)(2,1)}) %all-gather.5.cloned.1.call-update) | async-done | bytes 4194320 | tf_op jit(solution)/shard_map/all_gather | solution.py:117
  201.7 0.0 all-to-all-done
  201.7 0.0 copy-start.3
  201.7 1.8 convolution_convert_fusion.3
  203.6 1.7 convolution_convert_fusion.2
  205.3 0.0 copy-done.3
  205.3 0.5 convolution_convert_fusion.1
  205.7 0.5 convolution_convert_fusion
  206.2 1.7 add_convert_fusion
  (10 shorter events, 0.1 us)
Async XLA Ops:
  6.5 142.7 %copy-start = (bf16[2048,256]{1,0:T(8,128)(2,1)S(1)}, bf16[2048,256]{1,0:T(8,128)(2,1)}, u32[]{:S(2)}) copy-start(bf16[2048,256]{1,0:T(8,128)(2,1)} %param.11) | copy-start | bytes 3145732
  6.5 91.3 %copy-start.6 = (f32[2048]{0:T(1024)S(1)}, f32[2048]{0:T(1024)}, u32[]{:S(2)}) copy-start(f32[2048]{0:T(1024)} %param.10) | copy-start | bytes 24580
  6.5 74.5 %copy-start.7 = (s32[8]{0:T(128)S(1)}, s32[8]{0:T(128)}, u32[]{:S(2)}) copy-start(s32[8]{0:T(128)} %param.15) | copy-start | bytes 100
  6.5 88.0 %all-gather.3.cloned.1.call-start = ((), (), s32[]{:S(2)}) async-start(), calls=%async_computation.1 | async-start | bytes 5242880 | tf_op jit(solution)/shard_map/all_gather | solution.py:42
  7.3 194.5 %all-gather.5.cloned.1.call-start = ((), (), s32[]{:S(2)}) async-start(), calls=%async_computation.2 | async-start | bytes 5242880 | tf_op jit(solution)/shard_map/all_gather | solution.py:117
  94.6 3.4 %copy-start.2 = (bf16[1024,2048]{1,0:T(8,128)(2,1)S(1)}, bf16[1024,2048]{1,0:T(8,128)(2,1)}, u32[]{:S(2)}) copy-start(bf16[1024,2048]{1,0:T(8,128)(2,1)} %all-gather.3.cloned.1.call-done) | copy-start | bytes 12582916
  98.0 3.0 %copy-start.4 = (bf16[2048,64]{0,1:T(8,128)(2,1)S(1)}, bf16[2048,64]{0,1:T(8,128)(2,1)}, u32[]{:S(2)}) copy-start(bf16[2048,64]{0,1:T(8,128)(2,1)} %param.12) | copy-start | bytes 786436
  99.0 2.0 copy-start.1
  101.0 23.0 %copy-start.5 = (bf16[2048,64]{0,1:T(8,128)(2,1)S(1)}, bf16[2048,64]{0,1:T(8,128)(2,1)}, u32[]{:S(2)}) copy-start(bf16[2048,64]{0,1:T(8,128)(2,1)} %param.13) | copy-start | bytes 786436
  157.8 44.0 %all-to-all-start = ((bf16[4,256,256]{1,2,0:T(8,128)(2,1)}), bf16[4,256,256]{1,2,0:T(8,128)(2,1)S(1)}, u32[]{:S(2)}, u32[]{:S(2)}) async-start(bf16[4,256,256]{1,2,0:T(8,128)(2,1)} %copy.25), calls=%async_computation | async-start | bytes 1048576 | tf_op jit(solution)/shard_map/all_to_all | solution.py:116
  201.7 3.5 %copy-start.3 = (bf16[1024,2048]{1,0:T(8,128)(2,1)S(1)}, bf16[1024,2048]{1,0:T(8,128)(2,1)}, u32[]{:S(2)}) copy-start(bf16[1024,2048]{1,0:T(8,128)(2,1)} %all-gather.5.cloned.1.call-done) | copy-start | bytes 12582916
Sparse Core Ops, SparseCore 0:
  8.9 85.6 all-gather.2
  96.1 105.5 all-gather.4
where the time goes:
time: 215 us
  blocking collectives  113 us (53%)
  waiting for transfers between devices  53.3 us (25%)
  matrix products  16.8 us (8%)
  between operations  13.6 us (6%)
  other arithmetic  9.09 us (4%)
  starting transfers between devices  5.36 us (2%)
  local copies, waits for them, and re-layouts  3.97 us (2%)
    all_gather x1, waiting for transfers between devices, body(): full_out = lax.all_gather(w_out, 'tensor', axis=0, tiled=True)  38.6 us
    all_gather x1, blocking collectives, body(): lax.all_gather(prefix_value, ('cand', 'tensor'), axis=0, tiled=True)  27.9 us
    all_gather x1, blocking collectives, body(): lax.all_gather(prefix_key, ('cand', 'tensor'), axis=0, tiled=True)  26.7 us
    all_gather x1, blocking collectives, body(): lax.all_gather(cand_key, 'tensor', axis=1, tiled=True)  21.4 us
    all_gather x1, blocking collectives, body(): lax.all_gather(cand_value, 'tensor', axis=1, tiled=True)  21.3 us
    all_gather x1, blocking collectives, body(): lax.all_gather(prefix_states, 'tensor', axis=1, tiled=True)  15.3 us
    all_gather x1, waiting for transfers between devices, body(): lax.all_gather(cand_states, 'tensor', axis=1, tiled=True)  13.3 us
    all_to_all x1, starting transfers between devices, body(): lax.all_to_all(head_rows, 'tensor', split_axis=0, concat_axis=1, tiled=True)  5.32 us
  transfers between devices with their start and end apart: 3, of which 2 were waited for; matrix products, arithmetic and copies ran while one was open for 10% of the time, Pallas kernels for 0%

commit v1 on v0

--- a/solution.py
+++ b/solution.py
@@ -67,7 +67,7 @@
     ) * head_size ** (-0.5)
     queries = query_rows.astype(jnp.bfloat16).reshape(cand_count, cand_len, head_size)
     cand_key, cand_value = (
-        lax.all_gather(cand_key, "tensor", axis=1, tiled=True),
+        jnp.concatenate(lax.all_gather(cand_key, "tensor"), axis=1),
         lax.all_gather(cand_value, "tensor", axis=1, tiled=True),
     )
     key_pieces, value_pieces = (

time: 215 us -> 214 us (level)
  waiting for transfers between devices: 53.3 us -> 56.2 us
    all_gather x1, waiting for transfers between devices: 38.6 us -> 41.5 us  [body(): full_out = lax.all_gather(w_out, 'tensor', axis=0, tiled=True)]
where the time goes in v1:
time: 214 us
  blocking collectives  112 us (52%)
  waiting for transfers between devices  56.2 us (26%)
  matrix products  16.7 us (8%)
  between operations  13.7 us (6%)
  other arithmetic  9.1 us (4%)
  starting transfers between devices  3.68 us (2%)
  local copies, waits for them, and re-layouts  2.37 us (1%)
    all_gather x1, waiting for transfers between devices, body(): full_out = lax.all_gather(w_out, 'tensor', axis=0, tiled=True)  41.5 us
    all_gather x1, blocking collectives, body(): lax.all_gather(prefix_value, ('cand', 'tensor'), axis=0, tiled=True)  27.9 us
    all_gather x1, blocking collectives, body(): lax.all_gather(prefix_key, ('cand', 'tensor'), axis=0, tiled=True)  26.7 us
    all_gather x1, blocking collectives, body(): lax.all_gather(cand_value, 'tensor', axis=1, tiled=True)  22.5 us
    all_gather x1, blocking collectives, body(): lax.all_gather(cand_key, 'tensor')  19.6 us
    all_gather x1, blocking collectives, body(): lax.all_gather(prefix_states, 'tensor', axis=1, tiled=True)  15.3 us
    all_gather x1, waiting for transfers between devices, body(): lax.all_gather(cand_states, 'tensor', axis=1, tiled=True)  13.3 us
    dot_general x4, matrix products, body(): jnp.dot(all_heads[:, head_index * head_size:(head_index + 1) * head_size]...  4.42 us
  transfers between devices with their start and end apart: 3, of which 2 were waited for; matrix products, arithmetic and copies ran while one was open for 10% of the time, Pallas kernels for 0%

profile of v1, /device:TPU:0, one launch (start us, length us, event | category | flops | bytes accessed | tf_op | source)
XLA Modules:
  0.0 213.7 jit_solution(2698247154895858642)
XLA Ops:
  6.5 0.0 copy-start
  6.5 0.0 copy-start.6
  6.5 0.0 copy-start.7
  6.5 0.0 all-gather.4.cloned.1.call-start
  6.5 0.7 all-gather.4.cloned.1.call-update
  7.3 0.0 all-gather.6.cloned.1.call-start
  7.3 0.7 all-gather.6.cloned.1.call-update
  8.0 15.3 %all_gather.27 = bf16[32,2048]{1,0:T(8,128)(2,1)S(1)} all-gather(bf16[32,512]{1,0:T(8,128)(2,1)} %param.9), channel_id=1, replica_groups=mesh['query'=4,'cand'=2,'tensor'=4] {'tensor'}, dimensions={1}, use_global_device_ids=true | all-gather | bytes 163840 | tf_op jit(solution)/shard_map/all_gather | solution.py:43
  23.3 0.1 fusion.30
  23.5 1.2 convolution_convert_fusion.7
  24.7 26.7 %all_gather.28 = bf16[256,64]{1,0:T(8,128)(2,1)S(1)} all-gather(bf16[32,64]{1,0:T(8,128)(2,1)S(1)} %convolution_convert_fusion.7), channel_id=1, replica_groups=mesh['query'=4,'cand'=2,'tensor'=4] {'cand','tensor'}, dimensions={0}, use_global_device_ids=true | all-gather | bytes 36864 | tf_op jit(solution)/shard_map/all_gather | solution.py:74
  51.4 1.2 convolution_convert_fusion.6
  52.6 0.1 copy.17
  52.7 0.1 reshape.116
  52.9 27.9 %all_gather.30 = bf16[256,64]{1,0:T(8,128)(2,1)S(1)} all-gather(bf16[32,64]{1,0:T(8,128)(2,1)S(1)} %convolution_convert_fusion.6), channel_id=1, replica_groups=mesh['query'=4,'cand'=2,'tensor'=4] {'cand','tensor'}, dimensions={0}, use_global_device_ids=true | all-gather | bytes 36864 | tf_op jit(solution)/shard_map/all_gather | solution.py:75
  80.8 0.1 reshape.121
  81.0 0.0 copy-done.7
  81.0 0.1 iota_compare_fusion.1
  81.1 0.2 fusion.51
  81.3 13.3 %all-gather.4.cloned.1.call-done = bf16[1024,2048]{1,0:T(8,128)(2,1)} async-done(((bf16[1024,512]{1,0:T(8,128)(2,1)}), bf16[1024,2048]{1,0:T(8,128)(2,1)}) %all-gather.4.cloned.1.call-update) | async-done | bytes 4194320 | tf_op jit(solution)/shard_map/all_gather | solution.py:42
  94.6 0.0 copy-start.2
  94.6 3.2 %fusion = f32[1024]{0:T(1024)S(1)} fusion(bf16[1024,2048]{1,0:T(8,128)(2,1)} %all-gather.4.cloned.1.call-done), kind=kLoop, calls=%fused_computation.2 | loop fusion | flops 6290432 | bytes 4198400 | tf_op jit(solution)/shard_map/reduce_sum | solution.py:29
  97.8 0.0 copy-done.6
  97.8 0.2 copy-done.2
  98.0 0.0 copy-start.4
  98.0 1.0 fusion.2
  99.0 0.0 copy-done.4
  99.1 0.0 copy-start.1
  99.1 1.4 convolution_convert_fusion.5
  100.5 0.0 copy-start.5
  100.5 19.6 %all-gather = bf16[4096,64]{0,1:T(8,128)(2,1)S(1)} all-gather(bf16[1024,64]{0,1:T(8,128)(2,1)S(1)} %convolution_convert_fusion.5), channel_id=2, replica_groups=mesh['query'=4,'cand'=2,'tensor'=4] {'tensor'}, dimensions={0}, use_global_device_ids=true | all-gather | bytes 655360 | tf_op jit(solution)/shard_map/all_gather | solution.py:70
  120.0 0.1 convert_element_type.181
  120.1 0.1 copy.28
  120.2 0.0 copy-done.1
  120.2 0.1 fusion.65
  120.3 0.2 copy.24
  120.5 0.2 copy.25
  120.7 0.0 copy-done.5
  120.7 3.6 %convolution_convert_fusion.4 = bf16[1024,64]{0,1:T(8,128)(2,1)S(1)} fusion(bf16[1024,2048]{1,0:T(8,128)(2,1)} %copy-done.1, bf16[2048,64]{0,1:T(8,128)(2,1)S(1)} %copy-done.5), kind=kOutput, calls=%fused_computation.15 | convolution fusion | flops 268500992 | bytes 4587520 | tf_op jit(solution)/shard_map/dot_general | solution.py:56
  124.3 22.5 %all_gather.29 = bf16[1024,256]{0,1:T(8,128)(2,1)S(1)} all-gather(bf16[1024,64]{0,1:T(8,128)(2,1)S(1)} %convolution_convert_fusion.4), channel_id=1, replica_groups=mesh['query'=4,'cand'=2,'tensor'=4] {'tensor'}, dimensions={1}, use_global_device_ids=true | all-gather | bytes 655360 | tf_op jit(solution)/shard_map/all_gather | solution.py:71
  146.8 0.2 copy.23
  147.0 0.0 copy-done
  147.0 3.5 %fusion.68 = f32[1024,256]{1,0:T(8,128)S(1)} fusion(bf16[1024,2048]{1,0:T(8,128)(2,1)} %copy-done.1, bf16[2048,256]{1,0:T(8,128)(2,1)S(1)} %copy-done), kind=kOutput, calls=%fused_computation.94 | convolution fusion | flops 1073741824 | bytes 6291456 | tf_op jit(solution)/shard_map/dot_general | solution.py:66
  150.5 2.5 %fusion.19 = (f32[1024,128]{1,0:T(8,128)S(1)}, f32[1024,128]{1,0:T(8,128)S(1)}, bf16[1024,128]{1,0:T(8,128)(2,1)S(1)}, bf16[1024,128]{1,0:T(8,128)(2,1)S(1)}) fusion(f32[1024,256]{1,0:T(8,128)S(1)} %fusion.68, f32[128]{0:T(128)S(1)} %multiply_power_fusion, f32[1024]{0:T(1024)S(1)} %convert_bitcast_fusion.1, f32[1024,128]{1,0:T(8,128)S(1)} %copy.24, ...), kind=kLoop, calls=%fused_computation.36 | loop fusion | flops 1966080 | bytes 3674624 | tf_op jit(solution)/shard_map/sub | solution.py:20
  153.0 0.3 fusion.67
  153.3 0.3 fusion.66
  153.6 0.1 fusion.36
  153.7 0.1 fusion.28
  153.8 0.4 fusion.33
  154.2 0.4 fusion.5
  154.6 1.0 copy.21
  155.6 3.6 %all-to-all-start = ((bf16[4,256,256]{1,2,0:T(8,128)(2,1)}), bf16[4,256,256]{1,2,0:T(8,128)(2,1)S(1)}, u32[]{:S(2)}, u32[]{:S(2)}) async-start(bf16[4,256,256]{1,2,0:T(8,128)(2,1)} %copy.21), calls=%async_computation | async-start | bytes 1048576 | tf_op jit(solution)/shard_map/all_to_all | solution.py:116
  159.2 41.5 %all-gather.6.cloned.1.call-done = bf16[1024,2048]{1,0:T(8,128)(2,1)} async-done(((bf16[256,2048]{1,0:T(8,128)(2,1)}), bf16[1024,2048]{1,0:T(8,128)(2,1)}) %all-gather.6.cloned.1.call-update) | async-done | bytes 4194320 | tf_op jit(solution)/shard_map/all_gather | solution.py:117
  200.7 0.0 all-to-all-done
  200.7 0.0 copy-start.3
  200.7 1.8 convolution_convert_fusion.3
  202.6 1.7 convolution_convert_fusion.2
  204.3 0.0 copy-done.3
  204.3 0.5 convolution_convert_fusion.1
  204.7 0.5 convolution_convert_fusion
  205.2 1.7 add_convert_fusion
  (10 shorter events, 0.1 us)
Async XLA Ops:
  6.5 140.5 %copy-start = (bf16[2048,256]{1,0:T(8,128)(2,1)S(1)}, bf16[2048,256]{1,0:T(8,128)(2,1)}, u32[]{:S(2)}) copy-start(bf16[2048,256]{1,0:T(8,128)(2,1)} %param.11) | copy-start | bytes 3145732
  6.5 91.3 %copy-start.6 = (f32[2048]{0:T(1024)S(1)}, f32[2048]{0:T(1024)}, u32[]{:S(2)}) copy-start(f32[2048]{0:T(1024)} %param.10) | copy-start | bytes 24580
  6.5 74.5 %copy-start.7 = (s32[8]{0:T(128)S(1)}, s32[8]{0:T(128)}, u32[]{:S(2)}) copy-start(s32[8]{0:T(128)} %param.15) | copy-start | bytes 100
  6.5 88.0 %all-gather.4.cloned.1.call-start = ((), (), s32[]{:S(2)}) async-start(), calls=%async_computation.1 | async-start | bytes 5242880 | tf_op jit(solution)/shard_map/all_gather | solution.py:42
  7.3 193.5 %all-gather.6.cloned.1.call-start = ((), (), s32[]{:S(2)}) async-start(), calls=%async_computation.2 | async-start | bytes 5242880 | tf_op jit(solution)/shard_map/all_gather | solution.py:117
  94.6 3.4 %copy-start.2 = (bf16[1024,2048]{1,0:T(8,128)(2,1)S(1)}, bf16[1024,2048]{1,0:T(8,128)(2,1)}, u32[]{:S(2)}) copy-start(bf16[1024,2048]{1,0:T(8,128)(2,1)} %all-gather.4.cloned.1.call-done) | copy-start | bytes 12582916
  98.0 1.0 copy-start.4
  99.1 21.2 %copy-start.1 = (bf16[1024,2048]{1,0:T(8,128)(2,1)}, bf16[1024,2048]{1,0:T(8,128)(2,1)S(1)}, u32[]{:S(2)}) copy-start(bf16[1024,2048]{1,0:T(8,128)(2,1)S(1)} %fusion.2) | copy-start | bytes 12582916
  100.5 20.2 %copy-start.5 = (bf16[2048,64]{0,1:T(8,128)(2,1)S(1)}, bf16[2048,64]{0,1:T(8,128)(2,1)}, u32[]{:S(2)}) copy-start(bf16[2048,64]{0,1:T(8,128)(2,1)} %param.13) | copy-start | bytes 786436
  155.6 45.1 %all-to-all-start = ((bf16[4,256,256]{1,2,0:T(8,128)(2,1)}), bf16[4,256,256]{1,2,0:T(8,128)(2,1)S(1)}, u32[]{:S(2)}, u32[]{:S(2)}) async-start(bf16[4,256,256]{1,2,0:T(8,128)(2,1)} %copy.21), calls=%async_computation | async-start | bytes 1048576 | tf_op jit(solution)/shard_map/all_to_all | solution.py:116
  200.7 3.5 %copy-start.3 = (bf16[1024,2048]{1,0:T(8,128)(2,1)S(1)}, bf16[1024,2048]{1,0:T(8,128)(2,1)}, u32[]{:S(2)}) copy-start(bf16[1024,2048]{1,0:T(8,128)(2,1)} %all-gather.6.cloned.1.call-done) | copy-start | bytes 12582916
Sparse Core Ops, SparseCore 0:
  8.9 85.6 all-gather.3
  96.1 104.5 all-gather.5
